TPU v7x, 32 devices: a whole 2x2x4 slice. The times are simulated.
32 devices in a mesh: expert: 4 (over y, core), fsdp: 8 (over z, x).
Axes of the slice: x: 2, y: 2, z: 4, core: 2. Of those that a mesh axis runs over, the one named last changes fastest.
Arguments:
- layer_input: bfloat16 [8192, 2048], P(('expert', 'fsdp')), may hold values from -6 to 6
- expert_ids: int32 [8192, 8], P(('expert', 'fsdp')), may hold values from 0 to 15, as said below
- slot_ids: int32 [8192, 8], P(('expert', 'fsdp')), may hold values from 0 to 255, as said below
- attn_gain: float32 [2048], replicated, may hold values from 0.25 to 1.75
- qkv_weight: bfloat16 [2048, 6144], P('fsdp'), may hold values from -0.125 to 0.125
- query_gain: float32 [128], replicated, may hold values from 0.25 to 1.75
- key_gain: float32 [128], replicated, may hold values from 0.25 to 1.75
- out_weight: bfloat16 [2048, 2048], P('fsdp'), may hold values from -1 to 1
- ffn_gain: float32 [2048], replicated, may hold values from 0.25 to 1.75
- router_weight: bfloat16 [2048, 16], P('fsdp'), may hold values from -0.0625 to 0.0625
- gate_up_weight: bfloat16 [16, 2048, 2048], P('expert', 'fsdp'), may hold values from -0.125 to 0.125
- down_weight: bfloat16 [16, 1024, 2048], P('expert', 'fsdp'), may hold values from -0.75 to 0.75
- cotangent: bfloat16 [8192, 2048], P(('expert', 'fsdp')), may hold values from -6 to 6
Outputs:
- mixed_out: bfloat16 [8192, 2048], P(('expert', 'fsdp'))
- input_grad: float32 [8192, 2048], P(('expert', 'fsdp'))
- attn_gain_grad: float32 [2048], replicated
- qkv_weight_grad: float32 [2048, 6144], P('fsdp')
- query_gain_grad: float32 [128], replicated
- key_gain_grad: float32 [128], replicated
- out_weight_grad: float32 [2048, 2048], P('fsdp')
- ffn_gain_grad: float32 [2048], replicated
- router_weight_grad: float32 [2048, 16], P('fsdp')
- gate_up_grad: float32 [16, 2048, 2048], P('expert', 'fsdp')
- down_grad: float32 [16, 1024, 2048], P('expert', 'fsdp')
Inputs may be any that keep to these rules, and one draw needn't show every extreme that they name: `expert_ids`: each row names 8 different experts. Among the 256 rows of one device no expert is named more than 256 times; in every device's rows one expert is named exactly 256 times. `slot_ids`: among the rows of one device, the routes to one expert have different slots.
All inputs are finite; a program needn't handle non-finite values.
Results may differ from a plain program's by a relative error of at most 0.022.
Values may be sent and summed in bfloat16 or wider, within the bound.
No kernel may reach another device: no remote copies, remote signals or barrier semaphores. Data moves between devices by JAX's collectives and lax.ppermute only.
A program may use at most 384 MiB of HBM per device.

v0:
```python
import jax
import jax.numpy as jnp
from jax import lax
from jax.sharding import PartitionSpec as P

EPSILON = 1e-06
ROPE_BASE = 50000.0


def normalize(values):
    factor = lax.rsqrt(jnp.mean(values * values, -1, keepdims=True) + EPSILON)
    return (values * factor, factor)


def norm_back(grad_unit, unit_val, factor):
    return factor * (grad_unit - unit_val * jnp.mean(grad_unit * unit_val, -1, keepdims=True))


def tables(length, head_size):
    half_size = head_size // 2
    frequency = ROPE_BASE ** (-(jnp.arange(half_size, dtype=jnp.float32) * 2.0 / head_size))
    angles = jnp.arange(length, dtype=jnp.float32)[:, None] * frequency[None, :]
    angles = jnp.concatenate([angles, angles], 1)
    return (jnp.cos(angles)[:, None, :], jnp.sin(angles)[:, None, :])


def rotate(values, cos_table, sine_table):
    half_size = values.shape[-1] // 2
    turned = jnp.concatenate([-values[..., half_size:], values[..., :half_size]], -1)
    return values * cos_table + turned * sine_table


def rotate_back(gradient, cos_table, sine_table):
    half_size = gradient.shape[-1] // 2
    turned_grad = gradient * sine_table
    return gradient * cos_table + jnp.concatenate(
        [turned_grad[..., half_size:], -turned_grad[..., :half_size]], -1
    )


def local(
    layer_input,
    expert_ids,
    slot_ids,
    attn_gain,
    qkv_weight,
    query_gain,
    key_gain,
    out_weight,
    ffn_gain,
    router_weight,
    gate_up_weight,
    down_weight,
    cotangent,
):
    tokens, model_width = layer_input.shape
    top_count = expert_ids.shape[1]
    head_size = query_gain.shape[0]
    head_count = model_width // head_size
    experts = router_weight.shape[1]
    hidden = gate_up_weight.shape[2] // 2
    capacity = 2 * tokens * top_count // experts
    score_scale = head_size ** (-0.5)
    source = layer_input.astype(jnp.float32)
    unit_one, factor_one = normalize(source)
    normed = (unit_one * attn_gain).astype(jnp.bfloat16)
    qkv_full, out_full, router_full = (
        lax.all_gather(qkv_weight, "fsdp", axis=0, tiled=True),
        lax.all_gather(out_weight, "fsdp", axis=0, tiled=True),
        lax.all_gather(router_weight, "fsdp", axis=0, tiled=True),
    )
    projected = jnp.dot(normed, qkv_full, preferred_element_type=jnp.float32)
    queries = projected[:, :model_width].reshape(tokens, head_count, head_size)
    keys_raw = projected[:, model_width : 2 * model_width].reshape(tokens, head_count, head_size)
    values_raw = projected[:, 2 * model_width :].reshape(tokens, head_count, head_size)
    unit_query, factor_query = normalize(queries)
    unit_key, factor_key = normalize(keys_raw)
    cos_table, sine_table = tables(tokens, head_size)
    query_rot = rotate(unit_query * query_gain, cos_table, sine_table).astype(jnp.bfloat16)
    key_rot = rotate(unit_key * key_gain, cos_table, sine_table).astype(jnp.bfloat16)
    value_low = values_raw.astype(jnp.bfloat16)
    scores = (
        jnp.einsum("qhd,khd->hqk", query_rot, key_rot, preferred_element_type=jnp.float32)
        * score_scale
    )
    top_score = jnp.max(scores, -1, keepdims=True)
    weights_raw = jnp.exp(scores - top_score)
    totals = jnp.sum(weights_raw, -1, keepdims=True)
    log_total = top_score + jnp.log(totals)
    prob_low = (weights_raw / totals).astype(jnp.bfloat16)
    mixed_heads = jnp.einsum(
        "hqk,khd->qhd", prob_low, value_low, preferred_element_type=jnp.float32
    )
    mixed_low = mixed_heads.reshape(tokens, model_width).astype(jnp.bfloat16)
    residual = source + jnp.dot(mixed_low, out_full, preferred_element_type=jnp.float32)
    unit_two, factor_two = normalize(residual)
    normed_two = (unit_two * ffn_gain).astype(jnp.bfloat16)
    logits = jnp.dot(normed_two, router_full, preferred_element_type=jnp.float32)
    onehot = (expert_ids[:, :, None] == jnp.arange(experts, dtype=jnp.int32)[None, None, :]).astype(
        jnp.float32
    )
    chosen = jnp.sum(onehot * logits[:, None, :], -1)
    gate_probs = jax.nn.softmax(chosen, -1)
    slot_index = (expert_ids * capacity + slot_ids).reshape(-1)
    copies = jnp.broadcast_to(normed_two[:, None, :], (tokens, top_count, model_width)).reshape(
        tokens * top_count, model_width
    )
    outgoing = jnp.zeros((experts * capacity, model_width), jnp.bfloat16).at[slot_index].set(copies)
    arrived = lax.all_to_all(
        outgoing.reshape(experts, capacity, model_width),
        "expert",
        split_axis=0,
        concat_axis=1,
        tiled=True,
    )
    gate_up_full, down_full = (
        lax.all_gather(gate_up_weight, "fsdp", axis=1, tiled=True),
        lax.all_gather(down_weight, "fsdp", axis=1, tiled=True),
    )
    gate_up_val = jnp.einsum(
        "erd,edf->erf", arrived, gate_up_full, preferred_element_type=jnp.float32
    )
    gate_part = gate_up_val[..., :hidden]
    up_part = gate_up_val[..., hidden:]
    sigmoid_gate = jax.nn.sigmoid(gate_part)
    activated = (gate_part * sigmoid_gate * up_part).astype(jnp.bfloat16)
    expert_out = jnp.einsum(
        "erf,efd->erd", activated, down_full, preferred_element_type=jnp.float32
    ).astype(jnp.bfloat16)
    returned = lax.all_to_all(
        expert_out, "expert", split_axis=1, concat_axis=0, tiled=True
    ).reshape(experts * capacity, model_width)
    picked = returned[slot_index].reshape(tokens, top_count, model_width).astype(jnp.float32)
    moe_sum = jnp.sum(gate_probs[:, :, None] * picked, 1)
    mixed_out = (residual + moe_sum).astype(jnp.bfloat16)
    upstream = cotangent.astype(jnp.float32)
    gate_grad = jnp.sum(picked * upstream[:, None, :], -1)
    row_grad = (
        (gate_probs[:, :, None] * upstream[:, None, :])
        .astype(jnp.bfloat16)
        .reshape(tokens * top_count, model_width)
    )
    grad_out = (
        jnp.zeros((experts * capacity, model_width), jnp.bfloat16).at[slot_index].set(row_grad)
    )
    grad_arrived = lax.all_to_all(
        grad_out.reshape(experts, capacity, model_width),
        "expert",
        split_axis=0,
        concat_axis=1,
        tiled=True,
    )
    gate_up_back, down_back = (
        lax.all_gather(gate_up_weight, "fsdp", axis=1, tiled=True),
        lax.all_gather(down_weight, "fsdp", axis=1, tiled=True),
    )
    act_grad = jnp.einsum(
        "erd,efd->erf", grad_arrived, down_back, preferred_element_type=jnp.float32
    )
    down_grad_full = jnp.einsum(
        "erf,erd->efd", activated, grad_arrived, preferred_element_type=jnp.float32
    )
    gate_grad_part = act_grad * up_part * sigmoid_gate * (1.0 + gate_part * (1.0 - sigmoid_gate))
    up_grad_part = act_grad * gate_part * sigmoid_gate
    both_grad = jnp.concatenate([gate_grad_part, up_grad_part], -1).astype(jnp.bfloat16)
    gate_up_grad_full = jnp.einsum(
        "erd,erf->edf", arrived, both_grad, preferred_element_type=jnp.float32
    )
    input_rows = jnp.einsum(
        "erf,edf->erd", both_grad, gate_up_back, preferred_element_type=jnp.float32
    ).astype(jnp.bfloat16)
    rows_back = lax.all_to_all(
        input_rows, "expert", split_axis=1, concat_axis=0, tiled=True
    ).reshape(experts * capacity, model_width)
    gate_up_grad, down_grad = (
        lax.psum_scatter(
            gate_up_grad_full.astype(jnp.bfloat16), "fsdp", scatter_dimension=1, tiled=True
        ).astype(jnp.float32),
        lax.psum_scatter(
            down_grad_full.astype(jnp.bfloat16), "fsdp", scatter_dimension=1, tiled=True
        ).astype(jnp.float32),
    )
    mean_grad = jnp.sum(gate_probs * gate_grad, -1, keepdims=True)
    chosen_grad = gate_probs * (gate_grad - mean_grad)
    logit_grad = jnp.sum(onehot * chosen_grad[:, :, None], 1).astype(jnp.bfloat16)
    router_grad_full = jnp.dot(normed_two.T, logit_grad, preferred_element_type=jnp.float32)
    routed_back = jnp.sum(
        rows_back[slot_index].reshape(tokens, top_count, model_width).astype(jnp.float32), 1
    )
    normed_two_grad = routed_back + jnp.dot(
        logit_grad, router_full.T, preferred_element_type=jnp.float32
    )
    ffn_gain_part = jnp.sum(normed_two_grad * unit_two, 0)
    residual_grad = upstream + norm_back(normed_two_grad * ffn_gain, unit_two, factor_two)
    attn_grad_low = residual_grad.astype(jnp.bfloat16)
    out_grad_full = jnp.dot(mixed_low.T, attn_grad_low, preferred_element_type=jnp.float32)
    mixed_grad = jnp.dot(attn_grad_low, out_full.T, preferred_element_type=jnp.float32).astype(
        jnp.bfloat16
    )
    mixed_grad = mixed_grad.reshape(tokens, head_count, head_size)
    value_grad = jnp.einsum(
        "hqk,qhd->khd", prob_low, mixed_grad, preferred_element_type=jnp.float32
    )
    prob_grad = jnp.einsum(
        "qhd,khd->hqk", mixed_grad, value_low, preferred_element_type=jnp.float32
    )
    scores_again = (
        jnp.einsum("qhd,khd->hqk", query_rot, key_rot, preferred_element_type=jnp.float32)
        * score_scale
    )
    prob_full = jnp.exp(scores_again - log_total)
    score_grad = (
        prob_full * (prob_grad - jnp.sum(prob_full * prob_grad, -1, keepdims=True))
    ).astype(jnp.bfloat16)
    query_grad = (
        jnp.einsum("hqk,khd->qhd", score_grad, key_rot, preferred_element_type=jnp.float32)
        * score_scale
    )
    key_grad = (
        jnp.einsum("hqk,qhd->khd", score_grad, query_rot, preferred_element_type=jnp.float32)
        * score_scale
    )
    query_grad = rotate_back(query_grad, cos_table, sine_table)
    key_grad = rotate_back(key_grad, cos_table, sine_table)
    query_gain_part = jnp.sum(query_grad * unit_query, (0, 1))
    key_gain_part = jnp.sum(key_grad * unit_key, (0, 1))
    query_pre = norm_back(query_grad * query_gain, unit_query, factor_query)
    key_pre = norm_back(key_grad * key_gain, unit_key, factor_key)
    qkv_grad_low = jnp.concatenate(
        [
            query_pre.reshape(tokens, model_width),
            key_pre.reshape(tokens, model_width),
            value_grad.reshape(tokens, model_width),
        ],
        1,
    ).astype(jnp.bfloat16)
    qkv_grad_full = jnp.dot(normed.T, qkv_grad_low, preferred_element_type=jnp.float32)
    normed_grad = jnp.dot(qkv_grad_low, qkv_full.T, preferred_element_type=jnp.float32)
    attn_gain_part = jnp.sum(normed_grad * unit_one, 0)
    input_grad = residual_grad + norm_back(normed_grad * attn_gain, unit_one, factor_one)
    qkv_shard, out_shard, router_shard = (
        lax.psum_scatter(
            qkv_grad_full.astype(jnp.bfloat16), "fsdp", scatter_dimension=0, tiled=True
        ).astype(jnp.float32),
        lax.psum_scatter(
            out_grad_full.astype(jnp.bfloat16), "fsdp", scatter_dimension=0, tiled=True
        ).astype(jnp.float32),
        lax.psum_scatter(
            router_grad_full.astype(jnp.bfloat16), "fsdp", scatter_dimension=0, tiled=True
        ).astype(jnp.float32),
    )
    qkv_weight_grad, out_weight_grad, router_weight_grad = (
        lax.psum(qkv_shard.astype(jnp.bfloat16), "expert").astype(jnp.float32),
        lax.psum(out_shard.astype(jnp.bfloat16), "expert").astype(jnp.float32),
        lax.psum(router_shard.astype(jnp.bfloat16), "expert").astype(jnp.float32),
    )
    attn_gain_grad, query_gain_grad, key_gain_grad, ffn_gain_grad = lax.psum(
        (attn_gain_part, query_gain_part, key_gain_part, ffn_gain_part), ("expert", "fsdp")
    )
    return (
        mixed_out,
        input_grad,
        attn_gain_grad,
        qkv_weight_grad,
        query_gain_grad,
        key_gain_grad,
        out_weight_grad,
        ffn_gain_grad,
        router_weight_grad,
        gate_up_grad,
        down_grad,
    )


def solution(mesh):
    return jax.shard_map(
        local,
        mesh=mesh,
        in_specs=(
            P(("expert", "fsdp"), None),
            P(("expert", "fsdp"), None),
            P(("expert", "fsdp"), None),
            P(),
            P("fsdp", None),
            P(),
            P(),
            P("fsdp", None),
            P(),
            P("fsdp", None),
            P("expert", "fsdp", None),
            P("expert", "fsdp", None),
            P(("expert", "fsdp"), None),
        ),
        out_specs=(
            P(("expert", "fsdp"), None),
            P(("expert", "fsdp"), None),
            P(),
            P("fsdp", None),
            P(),
            P(),
            P("fsdp", None),
            P(),
            P("fsdp", None),
            P("expert", "fsdp", None),
            P("expert", "fsdp", None),
        ),
        check_vma=False,
    )
```

profile of v0, /device:TPU:0, one launch (start us, length us, event | category | flops | bytes accessed | tf_op | source)
XLA Modules:
  0.0 3566.4 jit_solution(18210329636455333657)
XLA Ops:
  9.7 1.5 convert_element_type.132
  11.3 67.9 %all_gather.19 = bf16[2048,16]{0,1:T(8,128)(2,1)S(1)} all-gather(bf16[256,16]{0,1:T(8,128)(2,1)S(1)} %copy-done.66), channel_id=1, replica_groups=mesh['expert'=4,'fsdp'=8] {'fsdp'}, dimensions={0}, use_global_device_ids=true | all-gather | bytes 73728 | tf_op jit(solution)/shard_map/all_gather | solution.py:70
  80.8 413.0 %all-gather.5.cloned.1.call-done = bf16[2048,6144]{1,0:T(8,128)(2,1)} async-done(((bf16[256,6144]{1,0:T(8,128)(2,1)}), bf16[2048,6144]{1,0:T(8,128)(2,1)}) %all-gather.5.cloned.1.call-update) | async-done | bytes 25165840 | tf_op jit(solution)/shard_map/all_gather | solution.py:68
  493.8 11.7 fusion.38
  505.5 1.9 slice_bitcast_fusion
  507.4 1.4 copy-done.20
  508.8 1.7 copy.226
  510.5 1.9 copy.188
  512.5 3.6 multiply_reduce_fusion.9
  517.1 3.3 copy.225
  520.4 3.4 copy.186
  523.8 2.9 multiply_reduce_fusion.10
  527.8 2.2 multiply_multiply_fusion
  535.6 2.1 convolution_convert_fusion.9
  537.7 83.1 %all-gather.7.cloned.1.call-done = bf16[2048,2048]{1,0:T(8,128)(2,1)} async-done(((bf16[256,2048]{1,0:T(8,128)(2,1)}), bf16[2048,2048]{1,0:T(8,128)(2,1)}) %all-gather.7.cloned.1.call-update) | async-done | bytes 8388624 | tf_op jit(solution)/shard_map/all_gather | solution.py:69
  620.8 5.8 multiply_reduce_fusion.8
  629.6 22.2 scatter_custom_fusion.1
  651.8 7.0 all-to-all-start.2
  659.4 21.2 scatter_custom_fusion
  680.6 161.2 %all-to-all-done.2 = bf16[16,256,2048]{2,1,0:T(8,128)(2,1)} async-done(((bf16[16,256,2048]{2,1,0:T(8,128)(2,1)}), bf16[16,256,2048]{2,1,0:T(8,128)(2,1)}, u32[]{:S(2)}, u32[]{:S(2)}) %all-to-all-start.2) | async-done | bytes 16777248 | tf_op jit(solution)/shard_map/all_to_all | solution.py:146
  841.9 7.6 all-to-all-start
  849.5 14.2 copy.199
  863.7 168.8 %all-to-all-done = bf16[16,256,2048]{2,1,0:T(8,128)(2,1)} async-done(((bf16[16,256,2048]{2,1,0:T(8,128)(2,1)}), bf16[16,256,2048]{2,1,0:T(8,128)(2,1)}, u32[]{:S(2)}, u32[]{:S(2)}) %all-to-all-start) | async-done | bytes 16777248 | tf_op jit(solution)/shard_map/all_to_all | solution.py:109
  1032.5 14.2 copy.195
  1046.7 211.6 %all-gather.9.cloned.1.call-done = bf16[4,2048,2048]{2,1,0:T(8,128)(2,1)} async-done(((bf16[4,256,2048]{2,1,0:T(8,128)(2,1)}), bf16[4,2048,2048]{2,1,0:T(8,128)(2,1)}) %all-gather.9.cloned.1.call-update) | async-done | bytes 33554448 | tf_op jit(solution)/shard_map/all_gather | solution.py:117
  1258.3 43.2 %fusion.53 = f32[4,1024,2048]{2,1,0:T(8,128)} fusion(bf16[4,1024,2048]{2,1,0:T(8,128)(2,1)} %bitcast.118, bf16[4,2048,2048]{2,1,0:T(8,128)(2,1)} %all-gather.9.cloned.1.call-done), kind=kOutput, calls=%fused_computation.138 | convolution fusion | flops 34359738368 | bytes 83886080 | tf_op jit(solution)/shard_map/erd,edf->erf/dot_general | solution.py:120
  1301.5 186.5 %all-gather.11.cloned.1.call-done = bf16[4,1024,2048]{2,1,0:T(8,128)(2,1)} async-done(((bf16[4,128,2048]{2,1,0:T(8,128)(2,1)}), bf16[4,1024,2048]{2,1,0:T(8,128)(2,1)}) %all-gather.11.cloned.1.call-update) | async-done | bytes 16777232 | tf_op jit(solution)/shard_map/all_gather | solution.py:118
  1488.0 37.0 %multiply_convert_fusion.1 = (bf16[4,1024,1024]{2,1,0:T(8,128)(2,1)}, bf16[4,1024,1024]{2,1,0:T(8,128)(2,1)}, bf16[4,1024,1024]{2,1,0:T(8,128)(2,1)}) fusion(f32[4,1024,2048]{2,1,0:T(8,128)} %fusion.53, bf16[4,1024,2048]{2,1,0:T(8,128)(2,1)} %bitcast.120, bf16[4,1024,2048]{2,1,0:T(8,128)(2,1)} %all-gather.11.cloned.1.call-done), kind=kOutput, calls=%fused_computation.15 | convolution fusion | flops 17246978048 | bytes 92274688 | tf_op jit(solution)/shard_map/erd,efd->erf/dot_general | solution.py:157
  1525.0 27.2 convolution_convert_fusion.4
  1552.2 22.1 copy.196
  1574.3 7.1 all-to-all-start.1
  1581.4 43.4 %convolution_convert_fusion.2 = bf16[4,1024,2048]{2,1,0:T(8,128)(2,1)} fusion(bf16[4,2048,2048]{2,1,0:T(8,128)(2,1)} %all-gather.9.cloned.1.call-done, bf16[4,1024,1024]{2,1,0:T(8,128)(2,1)} %get-tuple-element.30, bf16[4,1024,1024]{2,1,0:T(8,128)(2,1)} %get-tuple-element.29), kind=kOutput, calls=%fused_computation.18 | convolution fusion | flops 34401681408 | bytes 67108864 | tf_op jit(solution)/shard_map/erf,edf->erd/dot_general | solution.py:169
  1624.8 22.1 copy.202
  1646.9 117.5 %all-to-all-done.1 = bf16[4,1024,2048]{2,0,1:T(4,128)(2,1)} async-done(((bf16[4,1024,2048]{2,0,1:T(4,128)(2,1)}), bf16[4,1024,2048]{2,0,1:T(4,128)(2,1)}, u32[]{:S(2)}, u32[]{:S(2)}) %all-to-all-start.1) | async-done | bytes 16777248 | tf_op jit(solution)/shard_map/all_to_all | solution.py:130
  1764.5 7.2 all-to-all-start.3
  1771.8 18.6 copy.197
  1790.4 24.4 gather_fusion
  1814.8 9.5 fusion.1
  1824.5 130.2 %all-to-all-done.3 = bf16[4,1024,2048]{2,0,1:T(4,128)(2,1)} async-done(((bf16[4,1024,2048]{2,0,1:T(4,128)(2,1)}), bf16[4,1024,2048]{2,0,1:T(4,128)(2,1)}, u32[]{:S(2)}, u32[]{:S(2)}) %all-to-all-start.3) | async-done | bytes 16777248 | tf_op jit(solution)/shard_map/all_to_all | solution.py:172
  1954.7 18.6 copy.203
  1973.3 24.6 gather_fusion.1
  1998.0 11.4 convert_reduce_fusion
  2009.5 3.1 multiply_reduce_fusion.2
  2012.6 1.8 multiply_add_fusion
  2015.7 5.6 convolution_convert_fusion.5
  2022.9 6.1 convolution_convert_fusion.6
  2029.5 4.1 multiply_reduce_fusion
  2039.1 3.0 multiply_reduce_fusion.4
  2045.1 14.6 convolution_convert_fusion.1
  2061.9 27.1 convolution_convert_fusion.3
  2089.1 78.6 %reduce-scatter.8.cloned.1.call-done = bf16[256,2048]{1,0:T(8,128)(2,1)} async-done(((bf16[2048,2048]{1,0:T(8,128)(2,1)}), bf16[256,2048]{1,0:T(8,128)(2,1)}) %reduce-scatter.8.cloned.1.call-update) | async-done | bytes 1048592 | tf_op jit(solution)/shard_map/reduce_scatter | solution.py:245
  2167.7 407.0 %reduce-scatter.6.cloned.1.call-done = bf16[256,6144]{1,0:T(8,128)(2,1)} async-done(((bf16[2048,6144]{1,0:T(8,128)(2,1)}), bf16[256,6144]{1,0:T(8,128)(2,1)}) %reduce-scatter.6.cloned.1.call-update) | async-done | bytes 3145744 | tf_op jit(solution)/shard_map/reduce_scatter | solution.py:242
  2574.8 43.8 %convolution_convert_fusion = bf16[4,2048,2048]{2,1,0:T(8,128)(2,1)} fusion(bf16[4,1024,2048]{2,1,0:T(8,128)(2,1)} %bitcast.119, bf16[4,1024,1024]{2,1,0:T(8,128)(2,1)} %get-tuple-element.30, bf16[4,1024,1024]{2,1,0:T(8,128)(2,1)} %get-tuple-element.29), kind=kOutput, calls=%fused_computation.4 | convolution fusion | flops 34410070016 | bytes 67108864 | tf_op jit(solution)/shard_map/erd,erf->edf/dot_general | solution.py:166
  2618.7 14.2 fusion.22
  2633.0 43.8 %all-reduce = (f32[2048]{0:T(1024)}, f32[128]{0:T(128)}, f32[128]{0:T(128)}, f32[2048]{0:T(1024)}) all-reduce(f32[2048]{0:T(1024)S(1)} %get-tuple-element.19, f32[128]{0:T(128)S(1)} %copy-done.71, f32[128]{0:T(128)S(1)} %copy-done.72, f32[2048]{0:T(1024)S(1)} %copy-done.56), channel_id=1, replica_groups=mesh['expert'=4,'fsdp'=8] {'expert','fsdp'}, use_global_device_ids=true, to_apply=%region_22.0 | all-reduce | flops 4352 | bytes 34816 | tf_op jit(solution)/shard_map/psum | solution.py:257
  2676.8 3.5 fusion.21
  2680.2 6.7 psum.55
  2687.6 230.5 %reduce-scatter.14.cloned.1.call-done = bf16[4,128,2048]{2,1,0:T(8,128)(2,1)} async-done(((bf16[4,1024,2048]{2,1,0:T(8,128)(2,1)}), bf16[4,128,2048]{2,1,0:T(8,128)(2,1)}) %reduce-scatter.14.cloned.1.call-update) | async-done | bytes 2097168 | tf_op jit(solution)/shard_map/reduce_scatter | solution.py:179
  2918.1 4.1 convert_element_type.150
  2922.2 83.0 %all-reduce.4.cloned.1.call-done = (bf16[256,6144]{1,0:T(8,128)(2,1)}, bf16[256,2048]{1,0:T(8,128)(2,1)}) async-done(((bf16[256,6144]{1,0:T(8,128)(2,1)}, bf16[256,2048]{1,0:T(8,128)(2,1)}), (bf16[256,6144]{1,0:T(8,128)(2,1)}, bf16[256,2048]{1,0:T(8,128)(2,1)})) %all-reduce.4.cloned.1.call-update) | async-done | bytes 4194320 | tf_op jit(solution)/shard_map/psum | solution.py:253
  3005.3 2.9 convert_element_type.144
  3008.2 3.4 convert_element_type.142
  3011.6 541.0 %reduce-scatter.12.cloned.1.call-done = bf16[4,256,2048]{2,1,0:T(8,128)(2,1)} async-done(((bf16[4,2048,2048]{2,1,0:T(8,128)(2,1)}), bf16[4,256,2048]{2,1,0:T(8,128)(2,1)}) %reduce-scatter.12.cloned.1.call-update) | async-done | bytes 4194320 | tf_op jit(solution)/shard_map/reduce_scatter | solution.py:176
  3552.6 6.7 convert_element_type.148
  (215 shorter events, 29.8 us)
Async XLA Ops:
  7.2 486.6 %all-gather.5.cloned.1.call-start = ((), (), s32[]{:S(2)}) async-start(), calls=%async_computation.9 | async-start | bytes 28311552 | tf_op jit(solution)/shard_map/all_gather | solution.py:68
  7.2 2.2 copy-start.54
  7.2 2.2 copy-start.65
  7.2 2.5 copy-start.26
  7.9 3.4 copy-start.66
  7.9 612.9 %all-gather.7.cloned.1.call-start = ((), (), s32[]{:S(2)}) async-start(), calls=%async_computation.10 | async-start | bytes 9437184 | tf_op jit(solution)/shard_map/all_gather | solution.py:69
  8.7 71.8 %copy-start.14 = (bf16[256,2048]{1,0:T(8,128)(2,1)S(1)}, bf16[256,2048]{1,0:T(8,128)(2,1)}, u32[]{:S(2)}) copy-start(bf16[256,2048]{1,0:T(8,128)(2,1)} %param.13) | copy-start | bytes 3145732
  8.7 485.1 %copy-start.34 = (f32[2048]{0:T(1024)S(1)}, f32[2048]{0:T(1024)}, u32[]{:S(2)}) copy-start(f32[2048]{0:T(1024)} %param.16) | copy-start | bytes 24580
  8.7 1249.6 %all-gather.9.cloned.1.call-start = ((), (), s32[]{:S(2)}) async-start(), calls=%async_computation.11 | async-start | bytes 37748736 | tf_op jit(solution)/shard_map/all_gather | solution.py:117
  79.2 549.1 %copy-start.36 = (bf16[2048,16]{0,1:T(8,128)(2,1)}, bf16[2048,16]{0,1:T(8,128)(2,1)S(1)}, u32[]{:S(2)}) copy-start(bf16[2048,16]{0,1:T(8,128)(2,1)S(1)} %all_gather.19) | copy-start | bytes 196612
  80.8 424.7 %copy-start.50 = (f32[256]{0:T(256)}, f32[256]{0:T(256)S(1)}, u32[]{:S(2)}) copy-start(f32[256]{0:T(256)S(1)} %add_rsqrt_fusion.3) | copy-start | bytes 3076
  80.8 578.6 %copy-start.57 = (s32[2048,1]{0,1:T(1,128)}, s32[2048,1]{0,1:T(1,128)S(1)}, u32[]{:S(2)}) copy-start(s32[2048,1]{0,1:T(1,128)S(1)} %compare_select_fusion) | copy-start | bytes 24580
  505.5 3.3 copy-start.20
  512.5 15.3 copy-start.4
  520.4 7.3 copy-start.67
  520.4 7.4 copy-start.69
  527.7 2.3 copy-start.44
  527.7 2.2 copy-start.46
  537.7 83.1 %copy-start.18 = (bf16[16,128,256]{2,1,0:T(8,128)(2,1)}, bf16[16,128,256]{2,1,0:T(8,128)(2,1)S(1)}, u32[]{:S(2)}) copy-start(bf16[16,128,256]{2,1,0:T(8,128)(2,1)S(1)} %convolution_convert_fusion.9) | copy-start | bytes 3145732
  620.8 7.2 copy-start.52
  626.7 2.9 copy-start.10
  626.7 25.1 copy-start.61
  628.3 31.2 copy-start.16
  629.3 22.5 copy-start.63
  629.5 22.3 copy-start.32
  651.8 190.1 %all-to-all-start.2 = ((bf16[16,256,2048]{2,1,0:T(8,128)(2,1)}), bf16[16,256,2048]{2,1,0:T(8,128)(2,1)}, u32[]{:S(2)}, u32[]{:S(2)}) async-start(bf16[16,256,2048]{2,1,0:T(8,128)(2,1)} %bitcast.113), calls=%async_computation.2 | async-start | bytes 33554432 | tf_op jit(solution)/shard_map/all_to_all | solution.py:146
  658.8 829.2 %all-gather.11.cloned.1.call-start = ((), (), s32[]{:S(2)}) async-start(), calls=%async_computation.12 | async-start | bytes 18874368 | tf_op jit(solution)/shard_map/all_gather | solution.py:118
  841.9 190.6 %all-to-all-start = ((bf16[16,256,2048]{2,1,0:T(8,128)(2,1)}), bf16[16,256,2048]{2,1,0:T(8,128)(2,1)}, u32[]{:S(2)}, u32[]{:S(2)}) async-start(bf16[16,256,2048]{2,1,0:T(8,128)(2,1)} %bitcast.112), calls=%async_computation | async-start | bytes 33554432 | tf_op jit(solution)/shard_map/all_to_all | solution.py:109
  1574.3 190.1 %all-to-all-start.1 = ((bf16[4,1024,2048]{2,0,1:T(4,128)(2,1)}), bf16[4,1024,2048]{2,0,1:T(4,128)(2,1)}, u32[]{:S(2)}, u32[]{:S(2)}) async-start(bf16[4,1024,2048]{2,0,1:T(4,128)(2,1)} %copy.196), calls=%async_computation.1 | async-start | bytes 33554432 | tf_op jit(solution)/shard_map/all_to_all | solution.py:130
  1646.9 124.8 %copy-start.58 = (s32[2048,1]{0,1:T(1,128)S(1)}, s32[2048,1]{0,1:T(1,128)}, u32[]{:S(2)}) copy-start(s32[2048,1]{0,1:T(1,128)} %copy-done.57) | copy-start | bytes 24580
  1764.5 190.3 %all-to-all-start.3 = ((bf16[4,1024,2048]{2,0,1:T(4,128)(2,1)}), bf16[4,1024,2048]{2,0,1:T(4,128)(2,1)}, u32[]{:S(2)}, u32[]{:S(2)}) async-start(bf16[4,1024,2048]{2,0,1:T(4,128)(2,1)} %copy.202), calls=%async_computation.3 | async-start | bytes 33554432 | tf_op jit(solution)/shard_map/all_to_all | solution.py:172
  1771.7 396.0 %reduce-scatter.8.cloned.1.call-start = ((), (), s32[]{:S(2)}) async-start(), calls=%async_computation.14 | async-start | bytes 9437184 | tf_op jit(solution)/shard_map/reduce_scatter | solution.py:245
  1790.4 24.4 copy-start.11
  1790.4 24.4 copy-start.33
  1814.8 9.6 copy-start.41
  1814.8 9.6 copy-start.60
  1814.8 9.6 copy-start.64
  1814.8 9.6 copy-start.55
  1998.0 11.4 copy-start.3
  1998.0 11.4 copy-start.37
  1998.0 11.4 copy-start.53
  1998.0 11.4 copy-start.62
  2009.4 3.1 copy-start.25
  2009.4 3.1 copy-start.27
  2012.6 3.1 copy-start.19
  2021.3 553.5 %reduce-scatter.6.cloned.1.call-start = ((), (), s32[]{:S(2)}) async-start(), calls=%async_computation.13 | async-start | bytes 28311552 | tf_op jit(solution)/shard_map/reduce_scatter | solution.py:242
  2029.5 4.1 copy-start.1
  2036.9 2.2 copy-start.6
  2036.9 2.2 copy-start.38
  2036.9 2.2 copy-start.45
  2036.9 2.2 copy-start.47
  2036.9 2.2 copy-start.68
  2036.9 2.2 copy-start.70
  2039.1 3.0 copy-start.13
  2042.9 2.1 copy-start.15
  2059.8 620.5 %reduce-scatter.10.cloned.1.call-start = ((), (), s32[]{:S(2)}) async-start(), calls=%async_computation.15 | async-start | bytes 73728 | tf_op jit(solution)/shard_map/reduce_scatter | solution.py:248
  2061.8 856.2 %reduce-scatter.14.cloned.1.call-start = ((), (), s32[]{:S(2)}) async-start(), calls=%async_computation.17 | async-start | bytes 18874368 | tf_op jit(solution)/shard_map/reduce_scatter | solution.py:179
  2089.1 916.2 %all-reduce.4.cloned.1.call-start = ((), (), s32[]{:S(2)}) async-start(), calls=%async_computation.18 | async-start | bytes 8388608 | tf_op jit(solution)/shard_map/psum | solution.py:253
  2574.8 977.9 %reduce-scatter.12.cloned.1.call-start = ((), (), s32[]{:S(2)}) async-start(), calls=%async_computation.16 | async-start | bytes 37748736 | tf_op jit(solution)/shard_map/reduce_scatter | solution.py:176
  2618.7 14.3 copy-start.56
  2618.7 14.3 copy-start.71
  2618.7 14.3 copy-start.72
  2618.7 58.1 %copy-start.9 = (f32[256,2048]{1,0:T(8,128)S(1)}, f32[256,2048]{1,0:T(8,128)}, u32[]{:S(2)}) copy-start(f32[256,2048]{1,0:T(8,128)} %copy-done.7) | copy-start | bytes 6291460
  3005.3 2.9 copy-start.31
  (23 other events, 30.5 us)
Sparse Core Ops, SparseCore 0:
  9.5 484.1 all-gather.4
  495.9 124.8 all-gather.6
  622.4 635.9 all-gather.8
  1260.4 227.5 all-gather.10
  2021.4 146.2 reduce-scatter.7
  2171.9 402.7 reduce-scatter.5
  2578.2 52.8 reduce-scatter.9
  2635.3 282.7 reduce-scatter.13
  2920.5 84.6 all-reduce.3
  3009.3 543.2 reduce-scatter.11
where the time goes:
time: 3570 us
  waiting for transfers between devices  2810 us (79%)
  matrix products  293 us (8%)
  local copies, waits for them, and re-layouts  208 us (6%)
  blocking collectives  118 us (3%)
  other arithmetic  87 us (2%)
    reduce_scatter x1, waiting for transfers between devices, local(): lax.psum_scatter(gate_up_grad_full.astype(jnp.bfloat16), 'fsdp', scatter_...  541 us
    all_gather x1, waiting for transfers between devices, local(): lax.all_gather(qkv_weight, 'fsdp', axis=0, tiled=True)  413 us
    reduce_scatter x1, waiting for transfers between devices, local(): lax.psum_scatter(qkv_grad_full.astype(jnp.bfloat16), 'fsdp', scatter_dime...  407 us
    reduce_scatter x1, waiting for transfers between devices, local(): lax.psum_scatter(down_grad_full.astype(jnp.bfloat16), 'fsdp', scatter_dim...  231 us
    all_gather x1, waiting for transfers between devices, local(): lax.all_gather(gate_up_weight, 'fsdp', axis=1, tiled=True)  212 us
    all_gather x1, waiting for transfers between devices, local(): lax.all_gather(down_weight, 'fsdp', axis=1, tiled=True)  187 us
    all_to_all x1, waiting for transfers between devices, local(): lax.all_to_all(outgoing.reshape(experts, capacity, model_width), 'expert'...  169 us
    all_to_all x1, waiting for transfers between devices, local(): lax.all_to_all(grad_out.reshape(experts, capacity, model_width), 'expert'...  161 us
  transfers between devices with their start and end apart: 14, of which 13 were waited for; matrix products, arithmetic and copies ran while one was open for 12% of the time, Pallas kernels for 0%

commit v1 on v0

--- a/solution.py
+++ b/solution.py
@@ -5,6 +5,26 @@
 
 EPSILON = 1e-06
 ROPE_BASE = 50000.0
+
+
+def _define_meshes(local_values, dim_at):
+    full_n = jax.lax.axis_size("fsdp")
+    a_now = range(full_n)
+    work_now = map(lambda ii: (ii, (ii + 1) % full_n), a_now)
+    heap = list(work_now)
+    taken_in = range(full_n)
+    arr_out = map(lambda ii: (ii, (ii - 1) % full_n), taken_in)
+    pile = list(arr_out)
+    local_part, n_now = ([local_values], [local_values])
+    for _ in range(full_n // 2):
+        side_arr = jax.lax.ppermute(local_part[-1], "fsdp", heap)
+        local_part.append(side_arr)
+    for _ in range((full_n - 1) // 2):
+        top = jax.lax.ppermute(n_now[-1], "fsdp", pile)
+        n_now.append(top)
+    extra = jnp.concatenate([*local_part[::-1], *n_now[1:]], axis=dim_at)
+    x_next = jax.lax.axis_index("fsdp")
+    return jnp.roll(extra, (x_next - full_n // 2) * local_values.shape[dim_at], axis=dim_at)
 
 
 def normalize(values):
@@ -114,7 +134,7 @@
         tiled=True,
     )
     gate_up_full, down_full = (
-        lax.all_gather(gate_up_weight, "fsdp", axis=1, tiled=True),
+        _define_meshes(gate_up_weight, 1),
         lax.all_gather(down_weight, "fsdp", axis=1, tiled=True),
     )
     gate_up_val = jnp.einsum(

time: 3570 us -> 4260 us (1.19)
  blocking collectives: 118 us -> 432 us
  waiting for transfers between devices: 2810 us -> 3100 us
  local copies, waits for them, and re-layouts: 208 us -> 275 us
    ppermute x0 -> x7, waiting for transfers between devices: none -> 852 us  [the longest x3 490 us: _define_meshes(): top = jax.lax.ppermute(n_now[-1], 'fsdp', pile)]
    all_gather x1, blocking collectives: 67.9 us -> 383 us  [local(): lax.all_gather(router_weight, 'fsdp', axis=0, tiled=True)]
    all_gather x1, waiting for transfers between devices: 212 us -> 0.02 us  [local(): lax.all_gather(gate_up_weight, 'fsdp', axis=1, tiled=True)]
    all_gather x1, waiting for transfers between devices: 187 us -> 0.01 us  [local(): lax.all_gather(down_weight, 'fsdp', axis=1, tiled=True)]
    all_to_all x1, waiting for transfers between devices: 169 us -> 0.01 us  [local(): lax.all_to_all(outgoing.reshape(experts, capacity, model_width), 'expert'...]
    all_to_all x1, waiting for transfers between devices: 161 us -> 0.01 us  [local(): lax.all_to_all(grad_out.reshape(experts, capacity, model_width), 'expert'...]
    reduce_scatter x1, waiting for transfers between devices: 78.6 us -> 167 us  [local(): lax.psum_scatter(out_grad_full.astype(jnp.bfloat16), 'fsdp', scatter_dime...]
    all_gather x1, waiting for transfers between devices: 413 us -> 481 us  [local(): lax.all_gather(qkv_weight, 'fsdp', axis=0, tiled=True)]
  transfers between devices with their start and end apart: 14 -> 21, of which waited for: 13 -> 15; matrix products, arithmetic and copies ran while one was open for 12% -> 13% of each run, Pallas kernels for 0% -> 0%
where the time goes in v1:
time: 4260 us; the launch traced here: 4250 us
  waiting for transfers between devices  3100 us (73%)
  blocking collectives  432 us (10%)
  matrix products  294 us (7%)
  local copies, waits for them, and re-layouts  275 us (6%)
  other arithmetic  88 us (2%)
  starting transfers between devices  49.7 us (1%)
    reduce_scatter x1, waiting for transfers between devices, local(): lax.psum_scatter(gate_up_grad_full.astype(jnp.bfloat16), 'fsdp', scatter_...  540 us
    ppermute x3, waiting for transfers between devices, _define_meshes(): top = jax.lax.ppermute(n_now[-1], 'fsdp', pile)  490 us
    all_gather x1, waiting for transfers between devices, local(): lax.all_gather(qkv_weight, 'fsdp', axis=0, tiled=True)  481 us
    reduce_scatter x1, waiting for transfers between devices, local(): lax.psum_scatter(qkv_grad_full.astype(jnp.bfloat16), 'fsdp', scatter_dime...  407 us
    all_gather x1, blocking collectives, local(): lax.all_gather(router_weight, 'fsdp', axis=0, tiled=True)  383 us
    ppermute x4, waiting for transfers between devices, _define_meshes(): side_arr = jax.lax.ppermute(local_part[-1], 'fsdp', heap)  362 us
    reduce_scatter x1, waiting for transfers between devices, local(): lax.psum_scatter(down_grad_full.astype(jnp.bfloat16), 'fsdp', scatter_dim...  218 us
    reduce_scatter x1, waiting for transfers between devices, local(): lax.psum_scatter(out_grad_full.astype(jnp.bfloat16), 'fsdp', scatter_dime...  167 us
  transfers between devices with their start and end apart: 21, of which 15 were waited for; matrix products, arithmetic and copies ran while one was open for 13% of the time, Pallas kernels for 0%

profile of v1, /device:TPU:0, one launch (start us, length us, event | category | flops | bytes accessed | tf_op | source)
XLA Modules:
  0.0 4251.0 jit_solution(7285428233649535093)
XLA Ops:
  11.9 480.8 %all-gather.5.cloned.1.call-done = bf16[2048,6144]{1,0:T(8,128)(2,1)} async-done(((bf16[256,6144]{1,0:T(8,128)(2,1)}), bf16[2048,6144]{1,0:T(8,128)(2,1)}) %all-gather.5.cloned.1.call-update) | async-done | bytes 25165840 | tf_op jit(solution)/shard_map/all_gather | solution.py:88
  492.7 11.7 fusion.40
  533.9 85.8 %all-gather.7.cloned.1.call-done = bf16[2048,2048]{1,0:T(8,128)(2,1)} async-done(((bf16[256,2048]{1,0:T(8,128)(2,1)}), bf16[2048,2048]{1,0:T(8,128)(2,1)}) %all-gather.7.cloned.1.call-update) | async-done | bytes 8388624 | tf_op jit(solution)/shard_map/all_gather | solution.py:89
  619.8 5.8 multiply_reduce_fusion.8
  627.2 21.4 scatter_custom_fusion
  648.6 7.2 all-to-all-start
  656.4 177.6 %collective-permute-done = bf16[4,256,2048]{2,1,0:T(8,128)(2,1)S(1)} collective-permute-done((bf16[4,256,2048]{2,1,0:T(8,128)(2,1)}, bf16[4,256,2048]{2,1,0:T(8,128)(2,1)S(1)}, u32[]{:S(2)}, u32[]{:S(2)}) %collective-permute-start) | collective-permute-done | bytes 4194336 | tf_op jit(solution)/shard_map/ppermute | solution.py:20
  834.0 4.7 collective-permute-start.4
  838.7 179.5 %collective-permute-done.1 = bf16[4,256,2048]{2,1,0:T(8,128)(2,1)} collective-permute-done((bf16[4,256,2048]{2,1,0:T(8,128)(2,1)S(1)}, bf16[4,256,2048]{2,1,0:T(8,128)(2,1)}, u32[]{:S(2)}, u32[]{:S(2)}) %collective-permute-start.1) | collective-permute-done | bytes 4194336 | tf_op jit(solution)/shard_map/ppermute | solution.py:20
  1021.5 382.8 %all_gather.18 = bf16[2048,16]{0,1:T(8,128)(2,1)S(1)} all-gather(bf16[256,16]{0,1:T(8,128)(2,1)S(1)} %copy-done.69), channel_id=1, replica_groups=mesh['expert'=4,'fsdp'=8] {'fsdp'}, dimensions={0}, use_global_device_ids=true | all-gather | bytes 73728 | tf_op jit(solution)/shard_map/all_gather | solution.py:90
  1406.4 22.5 scatter_custom_fusion.1
  1428.9 7.0 all-to-all-start.2
  1438.0 351.1 %collective-permute-done.5 = bf16[4,256,2048]{2,1,0:T(8,128)(2,1)} collective-permute-done((bf16[4,256,2048]{2,1,0:T(8,128)(2,1)}, bf16[4,256,2048]{2,1,0:T(8,128)(2,1)}, u32[]{:S(2)}, u32[]{:S(2)}) %collective-permute-start.5) | collective-permute-done | bytes 4194336 | tf_op jit(solution)/shard_map/ppermute | solution.py:23
  1789.1 11.1 collective-permute-start.6
  1800.2 4.6 collective-permute-done.3
  1804.8 4.9 constant_dynamic-update-slice_fusion.15
  1809.7 4.9 constant_dynamic-update-slice_fusion.14
  1814.6 5.0 constant_dynamic-update-slice_fusion.13
  1825.7 4.9 constant_dynamic-update-slice_fusion.10
  1830.6 4.9 constant_dynamic-update-slice_fusion.9
  1835.5 138.8 %collective-permute-done.6 = bf16[4,256,2048]{2,1,0:T(8,128)(2,1)} collective-permute-done((bf16[4,256,2048]{2,1,0:T(8,128)(2,1)}, bf16[4,256,2048]{2,1,0:T(8,128)(2,1)}, u32[]{:S(2)}, u32[]{:S(2)}) %collective-permute-start.6) | collective-permute-done | bytes 4194336 | tf_op jit(solution)/shard_map/ppermute | solution.py:23
  1974.3 5.0 constant_dynamic-update-slice_fusion.8
  1979.3 5.0 constant_dynamic-update-slice_fusion.7
  1984.3 4.8 constant_dynamic-update-slice_fusion.6
  1989.2 4.8 constant_dynamic-update-slice_fusion.5
  1998.8 4.8 constant_dynamic-update-slice_fusion.2
  2003.6 4.8 constant_dynamic-update-slice_fusion.1
  2008.4 4.8 constant_dynamic-update-slice_fusion
  2013.3 14.3 copy.195
  2027.6 14.1 copy.199
  2041.7 43.2 %fusion = f32[4,1024,2048]{2,1,0:T(8,128)} fusion(bf16[4,1024,2048]{2,1,0:T(8,128)(2,1)} %bitcast.115, bf16[4,4096,2048]{2,1,0:T(8,128)(2,1)} %constant_dynamic-update-slice_fusion, s32[]{:T(128)S(6)} %select_n.28), kind=kOutput, calls=%fused_computation.4 | convolution fusion | flops 34359738368 | bytes 83886080 | tf_op jit(solution)/shard_map/erd,edf->erf/dot_general | solution.py:140
  2084.9 37.0 multiply_convert_fusion.1
  2121.9 27.3 convolution_convert_fusion.4
  2149.2 22.1 copy.196
  2171.3 7.0 all-to-all-start.1
  2178.3 43.3 %convolution_convert_fusion.2 = bf16[4,1024,2048]{2,1,0:T(8,128)(2,1)} fusion(bf16[4,2048,2048]{2,1,0:T(8,128)(2,1)} %all-gather.11.cloned.1.call-done, bf16[4,1024,1024]{2,1,0:T(8,128)(2,1)} %get-tuple-element.30, bf16[4,1024,1024]{2,1,0:T(8,128)(2,1)} %get-tuple-element.29), kind=kOutput, calls=%fused_computation.20 | convolution fusion | flops 34401681408 | bytes 67108864 | tf_op jit(solution)/shard_map/erf,edf->erd/dot_general | solution.py:189
  2221.6 22.2 copy.202
  2243.8 117.5 %all-to-all-done.1 = bf16[4,1024,2048]{2,0,1:T(4,128)(2,1)} async-done(((bf16[4,1024,2048]{2,0,1:T(4,128)(2,1)}), bf16[4,1024,2048]{2,0,1:T(4,128)(2,1)}, u32[]{:S(2)}, u32[]{:S(2)}) %all-to-all-start.1) | async-done | bytes 16777248 | tf_op jit(solution)/shard_map/all_to_all | solution.py:150
  2361.3 7.4 all-to-all-start.3
  2368.8 18.6 copy.197
  2387.5 24.4 gather_fusion
  2411.9 9.5 fusion.3
  2421.6 130.3 %all-to-all-done.3 = bf16[4,1024,2048]{2,0,1:T(4,128)(2,1)} async-done(((bf16[4,1024,2048]{2,0,1:T(4,128)(2,1)}), bf16[4,1024,2048]{2,0,1:T(4,128)(2,1)}, u32[]{:S(2)}, u32[]{:S(2)}) %all-to-all-start.3) | async-done | bytes 16777248 | tf_op jit(solution)/shard_map/all_to_all | solution.py:192
  2551.8 18.6 copy.203
  2570.4 24.4 gather_fusion.1
  2594.9 11.4 convert_reduce_fusion
  2612.6 5.6 convolution_convert_fusion.5
  2619.8 5.7 convolution_convert_fusion.6
  2626.1 4.0 multiply_reduce_fusion
  2641.6 14.6 convolution_convert_fusion.1
  2658.4 26.8 convolution_convert_fusion.3
  2685.3 166.7 %reduce-scatter.8.cloned.1.call-done = bf16[256,2048]{1,0:T(8,128)(2,1)} async-done(((bf16[2048,2048]{1,0:T(8,128)(2,1)}), bf16[256,2048]{1,0:T(8,128)(2,1)}) %reduce-scatter.8.cloned.1.call-update) | async-done | bytes 1048592 | tf_op jit(solution)/shard_map/reduce_scatter | solution.py:265
  2852.0 406.9 %reduce-scatter.6.cloned.1.call-done = bf16[256,6144]{1,0:T(8,128)(2,1)} async-done(((bf16[2048,6144]{1,0:T(8,128)(2,1)}), bf16[256,6144]{1,0:T(8,128)(2,1)}) %reduce-scatter.6.cloned.1.call-update) | async-done | bytes 3145744 | tf_op jit(solution)/shard_map/reduce_scatter | solution.py:262
  3259.0 43.9 %convolution_convert_fusion = bf16[4,2048,2048]{2,1,0:T(8,128)(2,1)} fusion(bf16[4,1024,2048]{2,1,0:T(8,128)(2,1)} %bitcast.116, bf16[4,1024,1024]{2,1,0:T(8,128)(2,1)} %get-tuple-element.30, bf16[4,1024,1024]{2,1,0:T(8,128)(2,1)} %get-tuple-element.29), kind=kOutput, calls=%fused_computation.6 | convolution fusion | flops 34410070016 | bytes 67108864 | tf_op jit(solution)/shard_map/erd,erf->edf/dot_general | solution.py:186
  3302.9 13.0 reduce-scatter.10.cloned.1.call-done
  3315.9 5.9 psum.55
  3322.4 14.9 fusion.24
  3337.3 43.8 %all-reduce = (f32[2048]{0:T(1024)}, f32[128]{0:T(128)}, f32[128]{0:T(128)}, f32[2048]{0:T(1024)}) all-reduce(f32[2048]{0:T(1024)S(1)} %get-tuple-element.19, f32[128]{0:T(128)S(1)} %copy-done.72, f32[128]{0:T(128)S(1)} %copy-done.73, f32[2048]{0:T(1024)S(1)} %copy-done.59), channel_id=1, replica_groups=mesh['expert'=4,'fsdp'=8] {'expert','fsdp'}, use_global_device_ids=true, to_apply=%region_22.23 | all-reduce | flops 4352 | bytes 34816 | tf_op jit(solution)/shard_map/psum | solution.py:277
  3384.6 218.3 %reduce-scatter.14.cloned.1.call-done = bf16[4,128,2048]{2,1,0:T(8,128)(2,1)} async-done(((bf16[4,1024,2048]{2,1,0:T(8,128)(2,1)}), bf16[4,128,2048]{2,1,0:T(8,128)(2,1)}) %reduce-scatter.14.cloned.1.call-update) | async-done | bytes 2097168 | tf_op jit(solution)/shard_map/reduce_scatter | solution.py:199
  3602.8 4.1 convert_element_type.150
  3607.0 83.0 %all-reduce.4.cloned.1.call-done = (bf16[256,6144]{1,0:T(8,128)(2,1)}, bf16[256,2048]{1,0:T(8,128)(2,1)}) async-done(((bf16[256,6144]{1,0:T(8,128)(2,1)}, bf16[256,2048]{1,0:T(8,128)(2,1)}), (bf16[256,6144]{1,0:T(8,128)(2,1)}, bf16[256,2048]{1,0:T(8,128)(2,1)})) %all-reduce.4.cloned.1.call-update) | async-done | bytes 4194320 | tf_op jit(solution)/shard_map/psum | solution.py:273
  3690.0 5.4 convert_element_type.142
  3697.0 540.3 %reduce-scatter.12.cloned.1.call-done = bf16[4,256,2048]{2,1,0:T(8,128)(2,1)} async-done(((bf16[4,2048,2048]{2,1,0:T(8,128)(2,1)}), bf16[4,256,2048]{2,1,0:T(8,128)(2,1)}) %reduce-scatter.12.cloned.1.call-update) | async-done | bytes 4194320 | tf_op jit(solution)/shard_map/reduce_scatter | solution.py:196
  4237.3 6.7 convert_element_type.148
  (247 shorter events, 82.1 us)
Async XLA Ops:
  7.2 485.5 %all-gather.5.cloned.1.call-start = ((), (), s32[]{:S(2)}) async-start(), calls=%async_computation.9 | async-start | bytes 28311552 | tf_op jit(solution)/shard_map/all_gather | solution.py:88
  7.9 3.6 copy-start.16
  7.9 611.8 %all-gather.7.cloned.1.call-start = ((), (), s32[]{:S(2)}) async-start(), calls=%async_computation.10 | async-start | bytes 9437184 | tf_op jit(solution)/shard_map/all_gather | solution.py:89
  8.7 484.0 %copy-start.37 = (f32[2048]{0:T(1024)S(1)}, f32[2048]{0:T(1024)}, u32[]{:S(2)}) copy-start(f32[2048]{0:T(1024)} %param.16) | copy-start | bytes 24580
  8.7 2076.2 %all-gather.9.cloned.1.call-start = ((), (), s32[]{:S(2)}) async-start(), calls=%async_computation.11 | async-start | bytes 18874368 | tf_op jit(solution)/shard_map/all_gather | solution.py:138
  9.4 2168.9 %all-gather.11.cloned.1.call-start = ((), (), s32[]{:S(2)}) async-start(), calls=%async_computation.12 | async-start | bytes 37748736 | tf_op jit(solution)/shard_map/all_gather | solution.py:174
  11.9 492.6 %copy-start.53 = (f32[256]{0:T(256)}, f32[256]{0:T(256)S(1)}, u32[]{:S(2)}) copy-start(f32[256]{0:T(256)S(1)} %add_rsqrt_fusion.3) | copy-start | bytes 3076
  11.9 1394.5 %copy-start.60 = (s32[2048,1]{0,1:T(1,128)}, s32[2048,1]{0,1:T(1,128)S(1)}, u32[]{:S(2)}) copy-start(s32[2048,1]{0,1:T(1,128)S(1)} %compare_select_fusion) | copy-start | bytes 24580
  504.4 3.3 copy-start.24
  508.2 5.3 copy-start.15
  515.9 10.3 copy-start.5
  523.2 3.0 copy-start.47
  524.0 2.3 copy-start.49
  533.9 91.7 %copy-start.22 = (bf16[16,128,256]{2,1,0:T(8,128)(2,1)}, bf16[16,128,256]{2,1,0:T(8,128)(2,1)S(1)}, u32[]{:S(2)}) copy-start(bf16[16,128,256]{2,1,0:T(8,128)(2,1)S(1)} %convolution_convert_fusion.9) | copy-start | bytes 3145732
  619.8 7.2 copy-start.55
  625.6 22.9 copy-start.64
  627.2 777.1 %copy-start.18 = (bf16[256,2048]{1,0:T(8,128)(2,1)}, bf16[256,2048]{1,0:T(8,128)(2,1)S(1)}, u32[]{:S(2)}) copy-start(bf16[256,2048]{1,0:T(8,128)(2,1)S(1)} %multiply_convert_fusion.6) | copy-start | bytes 3145732
  648.6 372.9 %copy-start.69 = (bf16[256,16]{0,1:T(8,128)(2,1)S(1)}, bf16[256,16]{0,1:T(8,128)(2,1)}, u32[]{:S(2)}) copy-start(bf16[256,16]{0,1:T(8,128)(2,1)} %param.22) | copy-start | bytes 24580
  648.6 780.3 %all-to-all-start = ((bf16[16,256,2048]{2,1,0:T(8,128)(2,1)}), bf16[16,256,2048]{2,1,0:T(8,128)(2,1)}, u32[]{:S(2)}, u32[]{:S(2)}) async-start(bf16[16,256,2048]{2,1,0:T(8,128)(2,1)} %bitcast.109), calls=%async_computation | async-start | bytes 33554432 | tf_op jit(solution)/shard_map/all_to_all | solution.py:129
  655.7 178.2 %collective-permute-start = (bf16[4,256,2048]{2,1,0:T(8,128)(2,1)}, bf16[4,256,2048]{2,1,0:T(8,128)(2,1)S(1)}, u32[]{:S(2)}, u32[]{:S(2)}) collective-permute-start(bf16[4,256,2048]{2,1,0:T(8,128)(2,1)} %param.23), channel_id=1, source_target_pairs={{0,1},{1,2},{2,3},{3,4},{4,5},{5,6},{6,7},{7,0},{8,9},{9,10},{10,1... | collective-permute-start | bytes 12582920 | tf_op jit(solution)/shard_map/ppermute | solution.py:20
  834.0 184.2 %copy-start.20 = (bf16[4,256,2048]{2,1,0:T(8,128)(2,1)}, bf16[4,256,2048]{2,1,0:T(8,128)(2,1)S(1)}, u32[]{:S(2)}) copy-start(bf16[4,256,2048]{2,1,0:T(8,128)(2,1)S(1)} %collective-permute-done) | copy-start | bytes 12582916
  834.0 184.2 %collective-permute-start.1 = (bf16[4,256,2048]{2,1,0:T(8,128)(2,1)S(1)}, bf16[4,256,2048]{2,1,0:T(8,128)(2,1)}, u32[]{:S(2)}, u32[]{:S(2)}) collective-permute-start(bf16[4,256,2048]{2,1,0:T(8,128)(2,1)S(1)} %collective-permute-done), channel_id=1, source_target_pairs={{0,1},{1,2},{2,3},{3,4},{4,5},{5,6},{6,7},{7,0},{8,9},{9,10},{10,1... | collective-permute-start | bytes 12582920 | tf_op jit(solution)/shard_map/ppermute | solution.py:20
  834.0 601.9 %collective-permute-start.4 = (bf16[4,256,2048]{2,1,0:T(8,128)(2,1)}, bf16[4,256,2048]{2,1,0:T(8,128)(2,1)}, u32[]{:S(2)}, u32[]{:S(2)}) collective-permute-start(bf16[4,256,2048]{2,1,0:T(8,128)(2,1)} %param.23), channel_id=1, source_target_pairs={{0,7},{1,0},{2,1},{3,2},{4,3},{5,4},{6,5},{7,6},{8,15},{9,8},{10,9... | collective-permute-start | bytes 12582920 | tf_op jit(solution)/shard_map/ppermute | solution.py:23
  1018.2 417.8 %collective-permute-start.2 = (bf16[4,256,2048]{2,1,0:T(8,128)(2,1)}, bf16[4,256,2048]{2,1,0:T(8,128)(2,1)}, u32[]{:S(2)}, u32[]{:S(2)}) collective-permute-start(bf16[4,256,2048]{2,1,0:T(8,128)(2,1)} %collective-permute-done.1), channel_id=1, source_target_pairs={{0,1},{1,2},{2,3},{3,4},{4,5},{5,6},{6,7},{7,0},{8,9},{9,10},{10,1... | collective-permute-start | bytes 12582920 | tf_op jit(solution)/shard_map/ppermute | solution.py:20
  1021.5 407.3 %copy-start.11 = (f32[256,2048]{1,0:T(8,128)}, f32[256,2048]{1,0:T(8,128)S(1)}, u32[]{:S(2)}) copy-start(f32[256,2048]{1,0:T(8,128)S(1)} %convert_element_type.132) | copy-start | bytes 6291460
  1406.2 22.6 copy-start.34
  1428.9 598.7 %all-to-all-start.2 = ((bf16[16,256,2048]{2,1,0:T(8,128)(2,1)}), bf16[16,256,2048]{2,1,0:T(8,128)(2,1)}, u32[]{:S(2)}, u32[]{:S(2)}) async-start(bf16[16,256,2048]{2,1,0:T(8,128)(2,1)} %bitcast.110), calls=%async_computation.2 | async-start | bytes 33554432 | tf_op jit(solution)/shard_map/all_to_all | solution.py:166
  1435.9 353.2 %collective-permute-start.5 = (bf16[4,256,2048]{2,1,0:T(8,128)(2,1)}, bf16[4,256,2048]{2,1,0:T(8,128)(2,1)}, u32[]{:S(2)}, u32[]{:S(2)}) collective-permute-start(bf16[4,256,2048]{2,1,0:T(8,128)(2,1)} %collective-permute-done.4), channel_id=1, source_target_pairs={{0,7},{1,0},{2,1},{3,2},{4,3},{5,4},{6,5},{7,6},{8,15},{9,8},{10,9... | collective-permute-start | bytes 12582920 | tf_op jit(solution)/shard_map/ppermute | solution.py:23
  1436.0 368.8 %collective-permute-start.3 = (bf16[4,256,2048]{2,1,0:T(8,128)(2,1)}, bf16[4,256,2048]{2,1,0:T(8,128)(2,1)}, u32[]{:S(2)}, u32[]{:S(2)}) collective-permute-start(bf16[4,256,2048]{2,1,0:T(8,128)(2,1)} %collective-permute-done.2), channel_id=1, source_target_pairs={{0,1},{1,2},{2,3},{3,4},{4,5},{5,6},{6,7},{7,0},{8,9},{9,10},{10,1... | collective-permute-start | bytes 12582920 | tf_op jit(solution)/shard_map/ppermute | solution.py:20
  1789.1 185.2 %collective-permute-start.6 = (bf16[4,256,2048]{2,1,0:T(8,128)(2,1)}, bf16[4,256,2048]{2,1,0:T(8,128)(2,1)}, u32[]{:S(2)}, u32[]{:S(2)}) collective-permute-start(bf16[4,256,2048]{2,1,0:T(8,128)(2,1)} %collective-permute-done.5), channel_id=1, source_target_pairs={{0,7},{1,0},{2,1},{3,2},{4,3},{5,4},{6,5},{7,6},{8,15},{9,8},{10,9... | collective-permute-start | bytes 12582920 | tf_op jit(solution)/shard_map/ppermute | solution.py:23
  1814.6 5.0 copy-start.21
  1819.6 3.7 copy-start.2
  2171.3 190.1 %all-to-all-start.1 = ((bf16[4,1024,2048]{2,0,1:T(4,128)(2,1)}), bf16[4,1024,2048]{2,0,1:T(4,128)(2,1)}, u32[]{:S(2)}, u32[]{:S(2)}) async-start(bf16[4,1024,2048]{2,0,1:T(4,128)(2,1)} %copy.196), calls=%async_computation.1 | async-start | bytes 33554432 | tf_op jit(solution)/shard_map/all_to_all | solution.py:150
  2243.8 125.0 %copy-start.61 = (s32[2048,1]{0,1:T(1,128)S(1)}, s32[2048,1]{0,1:T(1,128)}, u32[]{:S(2)}) copy-start(s32[2048,1]{0,1:T(1,128)} %copy-done.60) | copy-start | bytes 24580
  2361.3 190.5 %all-to-all-start.3 = ((bf16[4,1024,2048]{2,0,1:T(4,128)(2,1)}), bf16[4,1024,2048]{2,0,1:T(4,128)(2,1)}, u32[]{:S(2)}, u32[]{:S(2)}) async-start(bf16[4,1024,2048]{2,0,1:T(4,128)(2,1)} %copy.202), calls=%async_computation.3 | async-start | bytes 33554432 | tf_op jit(solution)/shard_map/all_to_all | solution.py:192
  2368.8 483.3 %reduce-scatter.8.cloned.1.call-start = ((), (), s32[]{:S(2)}) async-start(), calls=%async_computation.14 | async-start | bytes 9437184 | tf_op jit(solution)/shard_map/reduce_scatter | solution.py:265
  2387.5 24.4 copy-start.12
  2387.5 24.4 copy-start.35
  2411.9 9.6 copy-start.44
  2411.9 9.6 copy-start.63
  2411.9 9.6 copy-start.67
  2411.9 9.6 copy-start.58
  2594.9 11.4 copy-start.4
  2594.9 11.4 copy-start.40
  2594.9 11.4 copy-start.56
  2594.9 11.4 copy-start.65
  2606.3 3.1 copy-start.29
  2606.3 3.1 copy-start.30
  2609.5 3.1 copy-start.23
  2618.2 640.8 %reduce-scatter.6.cloned.1.call-start = ((), (), s32[]{:S(2)}) async-start(), calls=%async_computation.13 | async-start | bytes 28311552 | tf_op jit(solution)/shard_map/reduce_scatter | solution.py:262
  2626.1 4.1 copy-start.1
  2633.4 2.2 copy-start.7
  2633.4 2.2 copy-start.41
  2633.4 2.2 copy-start.48
  2635.6 3.0 copy-start.14
  2656.2 659.6 %reduce-scatter.10.cloned.1.call-start = ((), (), s32[]{:S(2)}) async-start(), calls=%async_computation.15 | async-start | bytes 73728 | tf_op jit(solution)/shard_map/reduce_scatter | solution.py:268
  2658.4 944.5 %reduce-scatter.14.cloned.1.call-start = ((), (), s32[]{:S(2)}) async-start(), calls=%async_computation.17 | async-start | bytes 18874368 | tf_op jit(solution)/shard_map/reduce_scatter | solution.py:199
  2685.3 1004.7 %all-reduce.4.cloned.1.call-start = ((), (), s32[]{:S(2)}) async-start(), calls=%async_computation.18 | async-start | bytes 8388608 | tf_op jit(solution)/shard_map/psum | solution.py:273
  3259.0 978.3 %reduce-scatter.12.cloned.1.call-start = ((), (), s32[]{:S(2)}) async-start(), calls=%async_computation.16 | async-start | bytes 37748736 | tf_op jit(solution)/shard_map/reduce_scatter | solution.py:196
  3322.4 14.9 copy-start.59
  3322.4 14.9 copy-start.72
  3322.4 14.9 copy-start.73
  3322.4 58.7 %copy-start.10 = (f32[256,2048]{1,0:T(8,128)S(1)}, f32[256,2048]{1,0:T(8,128)}, u32[]{:S(2)}) copy-start(f32[256,2048]{1,0:T(8,128)} %copy-done.8) | copy-start | bytes 6291460
  3690.0 5.4 copy-start.36
  (31 other events, 44.4 us)
Sparse Core Ops, SparseCore 0:
  9.5 483.1 all-gather.4
  494.8 124.8 all-gather.6
  622.0 443.4 all-gather.8
  1066.8 992.2 all-gather.10
  2618.3 233.6 reduce-scatter.7
  2856.3 402.6 reduce-scatter.5
  3263.0 52.8 reduce-scatter.9
  3320.1 282.6 reduce-scatter.13
  3605.3 84.6 all-reduce.3
  3694.0 543.1 reduce-scatter.11
